TPU v7x, 32 devices: a whole 2x2x4 slice. The times are simulated.
32 devices in a mesh: fsdp: 8 (over z, y), tensor: 4 (over x, core).
Axes of the slice: x: 2, y: 2, z: 4, core: 2. Of those that a mesh axis runs over, the one named last changes fastest.
Arguments:
- tokens: bfloat16 [64, 1024, 1024], P('fsdp', 'tensor'), may hold values from -6 to 6
- cotangent: bfloat16 [64, 1024, 1024], P('fsdp', 'tensor'), may hold values from -6 to 6
- routed_index: int32 [64, 128], P('fsdp'), may hold values from 0 to 1023, as said below
- query_weight: bfloat16 [1024, 1024], P('fsdp', 'tensor'), may hold values from -0.1875 to 0.1875
- key_weight: bfloat16 [1024, 1024], P('fsdp', 'tensor'), may hold values from -0.1875 to 0.1875
- value_weight: bfloat16 [1024, 1024], P('fsdp', 'tensor'), may hold values from -0.1875 to 0.1875
- output_weight: bfloat16 [1024, 1024], P('tensor', 'fsdp'), may hold values from -0.5 to 0.5
- up_weight: bfloat16 [1024, 4096], P('fsdp', 'tensor'), may hold values from -0.1875 to 0.1875
- down_weight: bfloat16 [4096, 1024], P('tensor', 'fsdp'), may hold values from -0.09375 to 0.09375
- router_weight: bfloat16 [1024], P('fsdp'), may hold values from -0.1875 to 0.1875
- attn_gain: bfloat16 [1024], P('fsdp'), may hold values from 0.5 to 1.5
- mlp_gain: bfloat16 [1024], P('fsdp'), may hold values from 0.5 to 1.5
Outputs:
- mixed: bfloat16 [64, 1024, 1024], P('fsdp', 'tensor')
- token_grad: bfloat16 [64, 1024, 1024], P('fsdp', 'tensor')
- query_weight_grad: float32 [1024, 1024], P('fsdp', 'tensor')
- key_weight_grad: float32 [1024, 1024], P('fsdp', 'tensor')
- value_weight_grad: float32 [1024, 1024], P('fsdp', 'tensor')
- output_weight_grad: float32 [1024, 1024], P('tensor', 'fsdp')
- up_weight_grad: float32 [1024, 4096], P('fsdp', 'tensor')
- down_weight_grad: float32 [4096, 1024], P('tensor', 'fsdp')
- router_weight_grad: float32 [1024], P('fsdp')
- attn_gain_grad: float32 [1024], P('fsdp')
- mlp_gain_grad: float32 [1024], P('fsdp')
Inputs may be any that keep to these rules, and one draw needn't show every extreme that they name: `routed_index`: each row holds 128 distinct positions of one sequence in ascending order; its first is 0 and its last is 1023.
All inputs are finite; a program needn't handle non-finite values.
Results may differ from a plain program's by a relative error of at most 0.011.
Values may be sent and summed in bfloat16 or wider, within the bound.
No kernel may reach another device: no remote copies, remote signals or barrier semaphores. Data moves between devices by JAX's collectives and lax.ppermute only.
A program may use at most 192 MiB of HBM per device.

v0:
```python
import jax
import jax.numpy as jnp
from jax import lax
from jax.sharding import PartitionSpec as P

HEAD_DIM = 64
BLOCK = 256
EPS = 1e-06
NEG = -1e30
HIGH = lax.Precision.HIGHEST


def pick_rows(values, routed_index, offset, pos_span):
    local_pos = routed_index - offset
    inside = (local_pos >= 0) & (local_pos < pos_span)
    safe_pos = jnp.clip(local_pos, 0, pos_span - 1)
    chosen = jnp.take_along_axis(values, safe_pos[:, :, None], axis=1).astype(jnp.float32)
    return jnp.where(inside[:, :, None], chosen, jnp.zeros_like(chosen))


def place_target(routed_index, offset, pos_span):
    local_pos = routed_index - offset
    inside = (local_pos >= 0) & (local_pos < pos_span)
    return jnp.where(inside, local_pos, pos_span)


def place_rows(values, new_rows, target):
    seq_ids = jnp.arange(values.shape[0], dtype=jnp.int32)[:, None]
    return values.at[seq_ids, target].set(new_rows, mode="drop")


def rms_scale(inputs):
    return lax.rsqrt(jnp.mean(inputs * inputs, axis=-1, keepdims=True) + EPS)


def norm_back(grad_out, inputs, scale_rows, gain):
    normal = inputs * scale_rows
    grad_norm = grad_out * gain
    grad_in = scale_rows * (
        grad_norm - normal * jnp.mean(grad_norm * normal, axis=-1, keepdims=True)
    )
    return (grad_in, jnp.sum(grad_out * normal, axis=0))


def attend_scores(query_heads, key_heads, allowed, score_scale):
    scores = (
        jnp.einsum("sqhe,skhe->shqk", query_heads, key_heads, preferred_element_type=jnp.float32)
        * score_scale
    )
    return jnp.where(allowed[:, None], scores, NEG)


def shards(
    tokens,
    cotangent,
    routed_index,
    query_weight,
    key_weight,
    value_weight,
    output_weight,
    up_weight,
    down_weight,
    router_weight,
    attn_gain,
    mlp_gain,
):
    tensor_count = lax.axis_size("tensor")
    tensor_rank = lax.axis_index("tensor")
    seq_count, pos_span, model_width = tokens.shape
    routed = routed_index.shape[1]
    share_rows = routed // tensor_count
    offset = tensor_rank * pos_span
    score_scale = HEAD_DIM ** (-0.5)
    strided = (seq_count, share_rows, tensor_count, model_width)
    mine = (seq_count, share_rows, 1, model_width)
    picked_tokens = pick_rows(tokens, routed_index, offset, pos_span).reshape(strided)
    picked_grads = pick_rows(cotangent, routed_index, offset, pos_span).reshape(strided)
    token_share, grad_share = (
        lax.psum_scatter(
            picked_tokens.astype(jnp.bfloat16), "tensor", scatter_dimension=2, tiled=True
        ).astype(jnp.float32),
        lax.psum_scatter(
            picked_grads.astype(jnp.bfloat16), "tensor", scatter_dimension=2, tiled=True
        ).astype(jnp.float32),
    )
    flat_tokens = token_share.reshape(-1, model_width)
    grad_flat = grad_share.reshape(-1, model_width)
    full_params = (
        lax.all_gather(query_weight, "fsdp", axis=0, tiled=True),
        lax.all_gather(key_weight, "fsdp", axis=0, tiled=True),
        lax.all_gather(value_weight, "fsdp", axis=0, tiled=True),
        lax.all_gather(output_weight, "fsdp", axis=1, tiled=True),
        lax.all_gather(up_weight, "fsdp", axis=0, tiled=True),
        lax.all_gather(down_weight, "fsdp", axis=1, tiled=True),
        lax.all_gather(router_weight, "fsdp", axis=0, tiled=True),
        lax.all_gather(attn_gain, "fsdp", axis=0, tiled=True),
        lax.all_gather(mlp_gain, "fsdp", axis=0, tiled=True),
    )
    (
        query_full,
        key_full,
        value_full,
        output_full,
        up_full,
        down_full,
        router_full,
        first_gain,
        second_gain,
    ) = full_params
    router_logit = jnp.dot(flat_tokens, router_full.astype(jnp.float32), precision=HIGH)
    gate_value = jax.nn.sigmoid(router_logit)
    first_scale = rms_scale(flat_tokens)
    first_normed = (flat_tokens * first_scale * first_gain.astype(jnp.float32)).astype(jnp.bfloat16)
    normed_all = lax.all_gather(first_normed.reshape(mine), "tensor", axis=2, tiled=True).reshape(
        -1, model_width
    )
    local_width = query_full.shape[1]
    heads_local = local_width // HEAD_DIM
    head_shape = (seq_count, routed, heads_local, HEAD_DIM)
    query_heads = (
        jnp.dot(normed_all, query_full, preferred_element_type=jnp.float32)
        .astype(jnp.bfloat16)
        .reshape(head_shape)
    )
    key_heads = (
        jnp.dot(normed_all, key_full, preferred_element_type=jnp.float32)
        .astype(jnp.bfloat16)
        .reshape(head_shape)
    )
    value_heads = (
        jnp.dot(normed_all, value_full, preferred_element_type=jnp.float32)
        .astype(jnp.bfloat16)
        .reshape(head_shape)
    )
    blocks = routed_index // BLOCK
    allowed = blocks[:, None, :] <= blocks[:, :, None]
    scores = attend_scores(query_heads, key_heads, allowed, score_scale)
    top_score = jnp.max(scores, axis=-1, keepdims=True)
    log_total = top_score + jnp.log(jnp.sum(jnp.exp(scores - top_score), axis=-1, keepdims=True))
    attn_probs = jnp.exp(scores - log_total).astype(jnp.bfloat16)
    context = (
        jnp.einsum("shqk,skhe->sqhe", attn_probs, value_heads, preferred_element_type=jnp.float32)
        .astype(jnp.bfloat16)
        .reshape(-1, local_width)
    )
    attn_part = jnp.dot(context, output_full, preferred_element_type=jnp.float32)
    attn_share = lax.psum_scatter(
        attn_part.reshape(strided), "tensor", scatter_dimension=2, tiled=True
    ).reshape(-1, model_width)
    hidden_in = flat_tokens + attn_share
    second_scale = rms_scale(hidden_in)
    second_gain_f = second_gain.astype(jnp.float32)
    second_normed = (hidden_in * second_scale * second_gain_f).astype(jnp.bfloat16)
    normed_mid = lax.all_gather(second_normed.reshape(mine), "tensor", axis=2, tiled=True).reshape(
        -1, model_width
    )
    up_value = jnp.dot(normed_mid, up_full, preferred_element_type=jnp.float32)
    activated = jax.nn.gelu(up_value).astype(jnp.bfloat16)
    mlp_part = jnp.dot(activated, down_full, preferred_element_type=jnp.float32)
    mlp_share = (
        lax.psum_scatter(
            mlp_part.reshape(strided).astype(jnp.bfloat16),
            "tensor",
            scatter_dimension=2,
            tiled=True,
        )
        .astype(jnp.float32)
        .reshape(-1, model_width)
    )
    branch = attn_share + mlp_share
    out_share = (flat_tokens + gate_value[:, None] * branch).astype(jnp.bfloat16)
    out_all = lax.all_gather(out_share.reshape(mine), "tensor", axis=2, tiled=True).reshape(
        seq_count, routed, model_width
    )
    target = place_target(routed_index, offset, pos_span)
    mixed = place_rows(tokens, out_all, target)
    back_params = (
        lax.all_gather(query_weight, "fsdp", axis=0, tiled=True),
        lax.all_gather(key_weight, "fsdp", axis=0, tiled=True),
        lax.all_gather(value_weight, "fsdp", axis=0, tiled=True),
        lax.all_gather(output_weight, "fsdp", axis=1, tiled=True),
        lax.all_gather(up_weight, "fsdp", axis=0, tiled=True),
        lax.all_gather(down_weight, "fsdp", axis=1, tiled=True),
        lax.all_gather(router_weight, "fsdp", axis=0, tiled=True),
        lax.all_gather(attn_gain, "fsdp", axis=0, tiled=True),
        lax.all_gather(mlp_gain, "fsdp", axis=0, tiled=True),
    )
    (
        query_back,
        key_back,
        value_back,
        output_back,
        up_back,
        down_back,
        router_back,
        first_gain_back,
        second_gain_back,
    ) = back_params
    gate_grad = jnp.sum(grad_flat * branch, axis=-1) * gate_value * (1.0 - gate_value)
    router_part = jnp.sum(flat_tokens * gate_grad[:, None], axis=0)
    branch_grad = gate_value[:, None] * grad_flat
    input_rows_grad = grad_flat + gate_grad[:, None] * router_back.astype(jnp.float32)
    mlp_grad_all = lax.all_gather(
        branch_grad.astype(jnp.bfloat16).reshape(mine), "tensor", axis=2, tiled=True
    ).reshape(-1, model_width)
    down_grad = jnp.einsum("rf,rd->fd", activated, mlp_grad_all, preferred_element_type=jnp.float32)
    act_grad = jnp.einsum("rd,fd->rf", mlp_grad_all, down_back, preferred_element_type=jnp.float32)
    gelu_out, gelu_back = jax.vjp(jax.nn.gelu, up_value)
    up_grad = gelu_back(act_grad)[0].astype(jnp.bfloat16)
    up_grad_weight = jnp.einsum(
        "rd,rf->df", normed_mid, up_grad, preferred_element_type=jnp.float32
    )
    mid_part = jnp.einsum("rf,df->rd", up_grad, up_back, preferred_element_type=jnp.float32)
    mid_share = lax.psum_scatter(
        mid_part.reshape(strided), "tensor", scatter_dimension=2, tiled=True
    ).reshape(-1, model_width)
    hidden_grad, second_gain_grad = norm_back(
        mid_share, hidden_in, second_scale, second_gain_back.astype(jnp.float32)
    )
    input_rows_grad = input_rows_grad + hidden_grad
    attn_grad_rows = (branch_grad + hidden_grad).astype(jnp.bfloat16)
    attn_grad_all = lax.all_gather(
        attn_grad_rows.reshape(mine), "tensor", axis=2, tiled=True
    ).reshape(-1, model_width)
    output_grad_weight = jnp.einsum(
        "rc,rd->cd", context, attn_grad_all, preferred_element_type=jnp.float32
    )
    context_grad = (
        jnp.einsum("rd,cd->rc", attn_grad_all, output_back, preferred_element_type=jnp.float32)
        .astype(jnp.bfloat16)
        .reshape(head_shape)
    )
    scores_again = attend_scores(query_heads, key_heads, allowed, score_scale)
    probs_exact = jnp.exp(scores_again - log_total)
    prob_grad = jnp.einsum(
        "sqhe,skhe->shqk", context_grad, value_heads, preferred_element_type=jnp.float32
    )
    value_grad = jnp.einsum(
        "shqk,sqhe->skhe",
        probs_exact.astype(jnp.bfloat16),
        context_grad,
        preferred_element_type=jnp.float32,
    ).astype(jnp.bfloat16)
    row_inner = jnp.sum(probs_exact * prob_grad, axis=-1, keepdims=True)
    score_grad = (probs_exact * (prob_grad - row_inner)).astype(jnp.bfloat16)
    query_grad = (
        (
            jnp.einsum("shqk,skhe->sqhe", score_grad, key_heads, preferred_element_type=jnp.float32)
            * score_scale
        )
        .astype(jnp.bfloat16)
        .reshape(-1, local_width)
    )
    key_grad = (
        (
            jnp.einsum(
                "shqk,sqhe->skhe", score_grad, query_heads, preferred_element_type=jnp.float32
            )
            * score_scale
        )
        .astype(jnp.bfloat16)
        .reshape(-1, local_width)
    )
    value_grad = value_grad.reshape(-1, local_width)
    query_grad_weight = jnp.einsum(
        "rd,rc->dc", normed_all, query_grad, preferred_element_type=jnp.float32
    )
    key_grad_weight = jnp.einsum(
        "rd,rc->dc", normed_all, key_grad, preferred_element_type=jnp.float32
    )
    value_grad_weight = jnp.einsum(
        "rd,rc->dc", normed_all, value_grad, preferred_element_type=jnp.float32
    )
    first_part = jnp.einsum("rc,dc->rd", query_grad, query_back, preferred_element_type=jnp.float32)
    first_part = first_part + jnp.einsum(
        "rc,dc->rd", key_grad, key_back, preferred_element_type=jnp.float32
    )
    first_part = first_part + jnp.einsum(
        "rc,dc->rd", value_grad, value_back, preferred_element_type=jnp.float32
    )
    first_share = lax.psum_scatter(
        first_part.reshape(strided), "tensor", scatter_dimension=2, tiled=True
    ).reshape(-1, model_width)
    norm_grad, first_gain_grad = norm_back(
        first_share, flat_tokens, first_scale, first_gain_back.astype(jnp.float32)
    )
    input_rows_grad = input_rows_grad + norm_grad
    vector_part = jnp.stack([router_part, first_gain_grad, second_gain_grad])
    rows_back, vector_all = (
        lax.all_gather(input_rows_grad.reshape(mine), "tensor", axis=2, tiled=True),
        lax.all_gather(vector_part, "tensor", axis=0, tiled=True),
    )
    vector_sum = jnp.sum(vector_all.reshape(tensor_count, 3, model_width), axis=0)
    token_grad = place_rows(
        cotangent, rows_back.reshape(seq_count, routed, model_width).astype(jnp.bfloat16), target
    )
    summed = (
        lax.psum_scatter(query_grad_weight, "fsdp", scatter_dimension=0, tiled=True),
        lax.psum_scatter(key_grad_weight, "fsdp", scatter_dimension=0, tiled=True),
        lax.psum_scatter(value_grad_weight, "fsdp", scatter_dimension=0, tiled=True),
        lax.psum_scatter(output_grad_weight, "fsdp", scatter_dimension=1, tiled=True),
        lax.psum_scatter(up_grad_weight, "fsdp", scatter_dimension=0, tiled=True),
        lax.psum_scatter(down_grad, "fsdp", scatter_dimension=1, tiled=True),
        lax.psum_scatter(vector_sum[0], "fsdp", scatter_dimension=0, tiled=True),
        lax.psum_scatter(vector_sum[1], "fsdp", scatter_dimension=0, tiled=True),
        lax.psum_scatter(vector_sum[2], "fsdp", scatter_dimension=0, tiled=True),
    )
    return (
        mixed,
        token_grad,
        summed[0],
        summed[1],
        summed[2],
        summed[3],
        summed[4],
        summed[5],
        summed[6],
        summed[7],
        summed[8],
    )


def solution(mesh):
    in_specs = (
        P("fsdp", "tensor", None),
        P("fsdp", "tensor", None),
        P("fsdp", None),
        P("fsdp", "tensor"),
        P("fsdp", "tensor"),
        P("fsdp", "tensor"),
        P("tensor", "fsdp"),
        P("fsdp", "tensor"),
        P("tensor", "fsdp"),
        P("fsdp"),
        P("fsdp"),
        P("fsdp"),
    )
    out_specs = (
        P("fsdp", "tensor", None),
        P("fsdp", "tensor", None),
        P("fsdp", "tensor"),
        P("fsdp", "tensor"),
        P("fsdp", "tensor"),
        P("tensor", "fsdp"),
        P("fsdp", "tensor"),
        P("tensor", "fsdp"),
        P("fsdp"),
        P("fsdp"),
        P("fsdp"),
    )
    return jax.shard_map(shards, mesh=mesh, in_specs=in_specs, out_specs=out_specs, check_vma=False)
```

profile of v0, /device:TPU:0, one launch (start us, length us, event | category | flops | bytes accessed | tf_op | source)
XLA Modules:
  0.0 1439.0 jit_solution(8234796519459619486)
XLA Ops:
  14.4 39.2 %gather_fusion = bf16[1024,1024]{1,0:T(8,128)(2,1)S(1)} fusion(bf16[8,256,1024]{2,1,0:T(8,128)(2,1)} %copy.187, s32[1024]{0:T(1024)S(1)} %or_bitcast_fusion), kind=kCustom, calls=%fused_computation.clone | custom fusion | bytes 4202496 | tf_op jit(solution)/shard_map/jit(take_along_axis)/gather | solution.py:17
  53.6 44.5 %gather_fusion.1 = bf16[1024,1024]{1,0:T(8,128)(2,1)} fusion(bf16[8,256,1024]{2,1,0:T(8,128)(2,1)} %copy.188, s32[1024]{0:T(1024)S(1)} %or_bitcast_fusion), kind=kCustom, calls=%fused_computation.1.clone | custom fusion | bytes 4202496 | tf_op jit(solution)/shard_map/jit(take_along_axis)/gather | solution.py:17
  110.1 21.4 %all-gather.1 = bf16[8,1,128]{2,1,0:T(2,128)(2,1)S(1)} all-gather(bf16[1,1,128]{2,1,0:T(2,128)(2,1)S(1)} %bitcast.220), channel_id=1, replica_groups=mesh['fsdp'=8,'tensor'=4] {'fsdp'}, dimensions={0}, use_global_device_ids=true | all-gather | bytes 2304 | tf_op jit(solution)/shard_map/all_gather | solution.py:96
  132.1 29.9 %all-reduce.17.cloned.1.call-done = bf16[8,32,4,1024]{3,1,2,0:T(8,128)(2,1)} async-done(((bf16[8,32,4,1024]{3,1,2,0:T(8,128)(2,1)}), bf16[8,32,4,1024]{3,1,2,0:T(8,128)(2,1)}) %all-reduce.17.cloned.1.call-update) | async-done | bytes 2097168
  166.1 31.6 %all_gather.61 = bf16[1024,256]{1,0:T(8,128)(2,1)S(1)} all-gather(bf16[128,256]{1,0:T(8,128)(2,1)S(1)} %copy-done.21), channel_id=1, replica_groups=mesh['fsdp'=8,'tensor'=4] {'fsdp'}, dimensions={0}, use_global_device_ids=true | all-gather | bytes 589824 | tf_op jit(solution)/shard_map/all_gather | solution.py:89
  197.7 31.5 %all_gather.62 = bf16[1024,256]{1,0:T(8,128)(2,1)S(1)} all-gather(bf16[128,256]{1,0:T(8,128)(2,1)S(1)} %copy-done.22), channel_id=1, replica_groups=mesh['fsdp'=8,'tensor'=4] {'fsdp'}, dimensions={0}, use_global_device_ids=true | all-gather | bytes 589824 | tf_op jit(solution)/shard_map/all_gather | solution.py:90
  229.1 33.5 %all_gather.60 = bf16[1024,256]{1,0:T(8,128)(2,1)} all-gather(bf16[128,256]{1,0:T(8,128)(2,1)S(1)} %copy-done.23), channel_id=1, replica_groups=mesh['fsdp'=8,'tensor'=4] {'fsdp'}, dimensions={0}, use_global_device_ids=true | all-gather | bytes 589824 | tf_op jit(solution)/shard_map/all_gather | solution.py:91
  262.6 28.6 %all_gather.63 = bf16[256,1024]{1,0:T(8,128)(2,1)} all-gather(bf16[256,128]{1,0:T(8,128)(2,1)S(1)} %copy-done.24), channel_id=1, replica_groups=mesh['fsdp'=8,'tensor'=4] {'fsdp'}, dimensions={1}, use_global_device_ids=true | all-gather | bytes 589824 | tf_op jit(solution)/shard_map/all_gather | solution.py:92
  317.5 19.0 %all-gather.2 = bf16[8,1,128]{2,1,0:T(2,128)(2,1)S(1)} all-gather(bf16[1,1,128]{2,1,0:T(2,128)(2,1)S(1)} %bitcast.221), channel_id=1, replica_groups=mesh['fsdp'=8,'tensor'=4] {'fsdp'}, dimensions={0}, use_global_device_ids=true | all-gather | bytes 2304 | tf_op jit(solution)/shard_map/all_gather | solution.py:97
  336.4 64.6 %all-reduce.19.cloned.1.call-done = f32[8,32,4,1024]{3,1,2,0:T(8,128)} async-done(((f32[8,32,4,1024]{3,1,2,0:T(8,128)}), f32[8,32,4,1024]{3,1,2,0:T(8,128)}) %all-reduce.19.cloned.1.call-update) | async-done | bytes 4194320
  435.7 42.7 %all-gather.17.cloned.1.call-done = bf16[1024,1024]{1,0:T(8,128)(2,1)} async-done(((bf16[128,1024]{1,0:T(8,128)(2,1)}), bf16[1024,1024]{1,0:T(8,128)(2,1)}) %all-gather.17.cloned.1.call-update) | async-done | bytes 2097168 | tf_op jit(solution)/shard_map/all_gather | solution.py:93
  485.0 45.0 %all-gather.19.cloned.1.call-done = bf16[1024,1024]{1,0:T(8,128)(2,1)} async-done(((bf16[1024,128]{1,0:T(8,128)(2,1)}), bf16[1024,1024]{1,0:T(8,128)(2,1)}) %all-gather.19.cloned.1.call-update) | async-done | bytes 2097168 | tf_op jit(solution)/shard_map/all_gather | solution.py:94
  545.3 17.6 %all-gather = bf16[8,1,128]{2,1,0:T(2,128)(2,1)S(1)} all-gather(bf16[1,1,128]{2,1,0:T(2,128)(2,1)S(1)} %bitcast.222), channel_id=1, replica_groups=mesh['fsdp'=8,'tensor'=4] {'fsdp'}, dimensions={0}, use_global_device_ids=true | all-gather | bytes 2304 | tf_op jit(solution)/shard_map/all_gather | solution.py:95
  564.1 64.5 %all-reduce.25.cloned.1.call-done = (bf16[8,32,4,1024]{3,1,2,0:T(8,128)(2,1)}, bf16[8,32,4,1024]{3,1,2,0:T(8,128)(2,1)}) async-done(((bf16[8,32,4,1024]{3,1,2,0:T(8,128)(2,1)}, bf16[8,32,4,1024]{3,1,2,0:T(8,128)(2,1)}), (bf16[8,32,4,1024]{3,1,2,0:T(8,128)(2,1)}, bf16[8,32,4,1024]{3,1,2,0:T(8,128)(2,1)})) %all-reduce.25.cloned.1.call-update) | async-done | bytes 4194320
  634.2 22.6 %all-gather.23.cloned.1.call-done = bf16[8,32,4,1024]{3,1,2,0:T(8,128)(2,1)} async-done(((bf16[8,32,1,1024]{3,1,2,0:T(8,128)(2,1)}), bf16[8,32,4,1024]{3,1,2,0:T(8,128)(2,1)}) %all-gather.23.cloned.1.call-update) | async-done | bytes 2097168 | tf_op jit(solution)/shard_map/all_gather | solution.py:203
  690.9 85.6 %all-reduce.21.cloned.1.call-done = f32[8,32,4,1024]{3,1,2,0:T(8,128)} async-done(((f32[8,32,4,1024]{3,1,2,0:T(8,128)}), f32[8,32,4,1024]{3,1,2,0:T(8,128)}) %all-reduce.21.cloned.1.call-update) | async-done | bytes 4194320
  782.4 22.4 %all-gather.25.cloned.1.call-done = bf16[8,32,4,1024]{3,1,2,0:T(8,128)(2,1)} async-done(((bf16[8,32,1,1024]{3,1,2,0:T(8,128)(2,1)}), bf16[8,32,4,1024]{3,1,2,0:T(8,128)(2,1)}) %all-gather.25.cloned.1.call-update) | async-done | bytes 2097168 | tf_op jit(solution)/shard_map/all_gather | solution.py:222
  844.4 85.5 %all-reduce.23.cloned.1.call-done = f32[8,32,4,1024]{3,1,2,0:T(8,128)} async-done(((f32[8,32,4,1024]{3,1,2,0:T(8,128)}), f32[8,32,4,1024]{3,1,2,0:T(8,128)}) %all-reduce.23.cloned.1.call-update) | async-done | bytes 4194320
  971.2 37.5 %all-reduce.9 = (f32[1024]{0:T(1024)S(1)}, f32[1024]{0:T(1024)S(1)}, f32[1024]{0:T(1024)S(1)}) all-reduce(f32[1024]{0:T(1024)S(1)} %bitcast.218, f32[1024]{0:T(1024)S(1)} %bitcast.217, f32[1024]{0:T(1024)S(1)} %bitcast.216), channel_id=14, replica_groups=mesh['fsdp'=8,'tensor'=4] {'fsdp'}, use_global_device_ids=true, to_apply=%region_26.28.clone | all-reduce | flops 3072 | bytes 24576
  1049.2 66.4 %reduce-scatter.29.cloned.1.call-done = f32[128,256]{1,0:T(8,128)} async-done(((f32[1024,256]{1,0:T(8,128)}), f32[128,256]{1,0:T(8,128)}) %reduce-scatter.29.cloned.1.call-update) | async-done | bytes 131088 | tf_op jit(solution)/shard_map/reduce_scatter | solution.py:300
  1115.6 66.7 %reduce-scatter.25.cloned.1.call-done = f32[128,256]{1,0:T(8,128)} async-done(((f32[1024,256]{1,0:T(8,128)}), f32[128,256]{1,0:T(8,128)}) %reduce-scatter.25.cloned.1.call-update) | async-done | bytes 131088 | tf_op jit(solution)/shard_map/reduce_scatter | solution.py:298
  1182.3 66.1 %reduce-scatter.27.cloned.1.call-done = f32[128,256]{1,0:T(8,128)} async-done(((f32[1024,256]{1,0:T(8,128)}), f32[128,256]{1,0:T(8,128)}) %reduce-scatter.27.cloned.1.call-update) | async-done | bytes 131088 | tf_op jit(solution)/shard_map/reduce_scatter | solution.py:299
  1248.5 91.9 %reduce-scatter.35.cloned.1.call-done = f32[1024,128]{1,0:T(8,128)} async-done(((f32[1024,1024]{1,0:T(8,128)}), f32[1024,128]{1,0:T(8,128)}) %reduce-scatter.35.cloned.1.call-update) | async-done | bytes 524304 | tf_op jit(solution)/shard_map/reduce_scatter | solution.py:303
  1340.3 91.9 %reduce-scatter.33.cloned.1.call-done = f32[128,1024]{1,0:T(8,128)} async-done(((f32[1024,1024]{1,0:T(8,128)}), f32[128,1024]{1,0:T(8,128)}) %reduce-scatter.33.cloned.1.call-update) | async-done | bytes 524304 | tf_op jit(solution)/shard_map/reduce_scatter | solution.py:302
  (222 shorter events, 273.3 us)
Async XLA Ops:
  7.2 154.9 %all-reduce.17.cloned.1.call-start = ((), (), s32[]{:S(2)}) async-start(), calls=%async_computation.20 | async-start | bytes 4194304
  109.5 88.2 %copy-start.22 = (bf16[128,256]{1,0:T(8,128)(2,1)S(1)}, bf16[128,256]{1,0:T(8,128)(2,1)}, u32[]{:S(2)}) copy-start(bf16[128,256]{1,0:T(8,128)(2,1)} %param.18) | copy-start | bytes 196612
  109.5 119.6 %copy-start.23 = (bf16[128,256]{1,0:T(8,128)(2,1)S(1)}, bf16[128,256]{1,0:T(8,128)(2,1)}, u32[]{:S(2)}) copy-start(bf16[128,256]{1,0:T(8,128)(2,1)} %param.19) | copy-start | bytes 196612
  109.5 181.7 %all-gather.13.cloned.1.call-start = ((), (), s32[]{:S(2)}) async-start(), calls=%async_computation.6 | async-start | bytes 2621440 | tf_op jit(solution)/shard_map/all_gather | solution.py:114
  162.1 100.5 %copy-start.24 = (bf16[256,128]{1,0:T(8,128)(2,1)S(1)}, bf16[256,128]{1,0:T(8,128)(2,1)}, u32[]{:S(2)}) copy-start(bf16[256,128]{1,0:T(8,128)(2,1)} %param.20) | copy-start | bytes 196612
  165.8 235.3 %all-reduce.19.cloned.1.call-start = ((), (), s32[]{:S(2)}) async-start(), calls=%async_computation.21 | async-start | bytes 8388608
  197.7 102.1 %copy-start.14 = (bf16[1024,256]{1,0:T(8,128)(2,1)}, bf16[1024,256]{1,0:T(8,128)(2,1)S(1)}, u32[]{:S(2)}) copy-start(bf16[1024,256]{1,0:T(8,128)(2,1)S(1)} %all_gather.61) | copy-start | bytes 1572868
  316.8 110.4 %all-gather.15.cloned.1.call-start = ((), (), s32[]{:S(2)}) async-start(), calls=%async_computation.7 | async-start | bytes 2621440 | tf_op jit(solution)/shard_map/all_gather | solution.py:154
  404.3 74.2 %all-gather.17.cloned.1.call-start = ((), (), s32[]{:S(2)}) async-start(), calls=%async_computation.8 | async-start | bytes 2359296 | tf_op jit(solution)/shard_map/all_gather | solution.py:93
  404.9 125.1 %all-gather.19.cloned.1.call-start = ((), (), s32[]{:S(2)}) async-start(), calls=%async_computation.9 | async-start | bytes 2359296 | tf_op jit(solution)/shard_map/all_gather | solution.py:94
  405.5 223.2 %all-reduce.25.cloned.1.call-start = ((), (), s32[]{:S(2)}) async-start(), calls=%async_computation.24 | async-start | bytes 8388608
  544.7 112.2 %all-gather.23.cloned.1.call-start = ((), (), s32[]{:S(2)}) async-start(), calls=%async_computation.11 | async-start | bytes 2621440 | tf_op jit(solution)/shard_map/all_gather | solution.py:203
  633.9 142.6 %all-reduce.21.cloned.1.call-start = ((), (), s32[]{:S(2)}) async-start(), calls=%async_computation.22 | async-start | bytes 8388608
  690.9 114.0 %all-gather.25.cloned.1.call-start = ((), (), s32[]{:S(2)}) async-start(), calls=%async_computation.12 | async-start | bytes 2621440 | tf_op jit(solution)/shard_map/all_gather | solution.py:222
  782.0 147.9 %all-reduce.23.cloned.1.call-start = ((), (), s32[]{:S(2)}) async-start(), calls=%async_computation.23 | async-start | bytes 8388608
  844.2 85.7 %copy-start.1 = (bf16[8,32,1,1024]{3,1,2,0:T(8,128)(2,1)S(1)}, bf16[8,32,1,1024]{3,1,2,0:T(8,128)(2,1)}, u32[]{:S(2)}) copy-start(bf16[8,32,1,1024]{3,1,2,0:T(8,128)(2,1)} %copy-done) | copy-start | bytes 1572868
  844.2 166.2 %all-gather.21.cloned.1.call-start = ((), (), s32[]{:S(2)}) async-start(), calls=%async_computation.10 | async-start | bytes 2621440 | tf_op jit(solution)/shard_map/all_gather | solution.py:172
  933.6 84.0 %all-gather.27.cloned.1.call-start = ((), (), s32[]{:S(2)}) async-start(), calls=%async_computation.13 | async-start | bytes 2621440 | tf_op jit(solution)/shard_map/all_gather | solution.py:290
  937.8 111.4 %reduce-scatter.31.cloned.1.call-start = ((), (), s32[]{:S(2)}) async-start(), calls=%async_computation.17 | async-start | bytes 1179648 | tf_op jit(solution)/shard_map/reduce_scatter | solution.py:301
  941.7 173.8 %reduce-scatter.29.cloned.1.call-start = ((), (), s32[]{:S(2)}) async-start(), calls=%async_computation.16 | async-start | bytes 1179648 | tf_op jit(solution)/shard_map/reduce_scatter | solution.py:300
  944.7 237.7 %reduce-scatter.25.cloned.1.call-start = ((), (), s32[]{:S(2)}) async-start(), calls=%async_computation.14 | async-start | bytes 1179648 | tf_op jit(solution)/shard_map/reduce_scatter | solution.py:298
  946.5 302.0 %reduce-scatter.27.cloned.1.call-start = ((), (), s32[]{:S(2)}) async-start(), calls=%async_computation.15 | async-start | bytes 1179648 | tf_op jit(solution)/shard_map/reduce_scatter | solution.py:299
  948.3 392.0 %reduce-scatter.35.cloned.1.call-start = ((), (), s32[]{:S(2)}) async-start(), calls=%async_computation.19 | async-start | bytes 4718592 | tf_op jit(solution)/shard_map/reduce_scatter | solution.py:303
  956.0 476.1 %reduce-scatter.33.cloned.1.call-start = ((), (), s32[]{:S(2)}) async-start(), calls=%async_computation.18 | async-start | bytes 4718592 | tf_op jit(solution)/shard_map/reduce_scatter | solution.py:302
  (30 other events, 213.5 us)
Sparse Core Ops, SparseCore 0:
  109.6 52.3 all-reduce.16
  165.9 22.6 all-gather.12
  316.9 84.0 all-reduce.18
  404.4 22.7 all-gather.14
  429.2 49.2 all-gather.16
  480.4 49.5 all-gather.18
  544.8 83.8 all-reduce.24
  634.1 22.7 all-gather.22
  691.0 85.4 all-reduce.20
  782.1 22.7 all-gather.24
  844.4 85.4 all-reduce.22
  933.8 22.7 all-gather.20
  958.2 22.9 all-gather.26
  985.3 63.8 reduce-scatter.30
  1053.0 62.4 reduce-scatter.28
  1119.8 62.4 reduce-scatter.24
  1186.1 62.2 reduce-scatter.26
  1253.0 87.3 reduce-scatter.34
  1344.5 87.6 reduce-scatter.32
where the time goes:
time: 1450 us; the launch traced here: 1440 us
  waiting for transfers between devices  866 us (60%)
  blocking collectives  226 us (16%)
  local copies, waits for them, and re-layouts  221 us (15%)
  matrix products  74.1 us (5%)
  other arithmetic  34.6 us (2%)
  between operations  15.4 us (1%)
    unnamed x24, waiting for transfers between devices  332 us
    reduce_scatter x1, waiting for transfers between devices, shards(): lax.psum_scatter(up_grad_weight, 'fsdp', scatter_dimension=0, tiled=True)  91.9 us
    reduce_scatter x1, waiting for transfers between devices, shards(): lax.psum_scatter(down_grad, 'fsdp', scatter_dimension=1, tiled=True)  91.9 us
    gather x2, local copies, waits for them, and re-layouts, pick_rows(): jnp.take_along_axis(values, safe_pos[:, :, None], axis=1)  83.7 us
    reduce_scatter x1, waiting for transfers between devices, shards(): lax.psum_scatter(query_grad_weight, 'fsdp', scatter_dimension=0, tiled=True)  66.7 us
    reduce_scatter x1, waiting for transfers between devices, shards(): lax.psum_scatter(value_grad_weight, 'fsdp', scatter_dimension=0, tiled=True)  66.4 us
    reduce_scatter x1, waiting for transfers between devices, shards(): lax.psum_scatter(key_grad_weight, 'fsdp', scatter_dimension=0, tiled=True)  66.1 us
    all_gather x1, waiting for transfers between devices, shards(): lax.all_gather(down_weight, 'fsdp', axis=1, tiled=True)  45 us
  transfers between devices with their start and end apart: 19, of which 16 were waited for; matrix products, arithmetic and copies ran while one was open for 6% of the time, Pallas kernels for 0%

commit v1 on v0

--- a/solution.py
+++ b/solution.py
@@ -85,10 +85,24 @@
     )
     flat_tokens = token_share.reshape(-1, model_width)
     grad_flat = grad_share.reshape(-1, model_width)
+
+    def row_draft(chunk):
+        taken_in = lax.axis_size("fsdp")
+        z_new = lax.axis_index("fsdp")
+        top, placed = (taken_in, z_new)
+        now, later = (chunk, 1)
+        while later < top:
+            x_next = lax.ppermute(now, "fsdp", [(c, c ^ later) for c in range(top)])
+            state_now = jnp.concatenate([now, x_next], 0)
+            m_next = jnp.concatenate([x_next, now], 0)
+            now = jnp.where(placed & later == 0, state_now, m_next)
+            later = 2 * later
+        return now
+
     full_params = (
         lax.all_gather(query_weight, "fsdp", axis=0, tiled=True),
         lax.all_gather(key_weight, "fsdp", axis=0, tiled=True),
-        lax.all_gather(value_weight, "fsdp", axis=0, tiled=True),
+        row_draft(value_weight),
         lax.all_gather(output_weight, "fsdp", axis=1, tiled=True),
         lax.all_gather(up_weight, "fsdp", axis=0, tiled=True),
         lax.all_gather(down_weight, "fsdp", axis=1, tiled=True),

time: 1450 us -> 1440 us (level)
  waiting for transfers between devices: 866 us -> 851 us
    all_gather x1, waiting for transfers between devices: 22.4 us -> 0.01 us  [shards(): lax.all_gather(attn_grad_rows.reshape(mine), 'tensor', axis=2, tiled=True)]
    unnamed x79 -> x77, local copies, waits for them, and re-layouts: 38.3 us -> 38.2 us
  transfers between devices with their start and end apart: 19 -> 22, of which waited for: 16 -> 16; matrix products, arithmetic and copies ran while one was open for 6% -> 7% of each run, Pallas kernels for 0% -> 0%
where the time goes in v1:
time: 1440 us; the launch traced here: 1430 us
  waiting for transfers between devices  851 us (59%)
  blocking collectives  229 us (16%)
  local copies, waits for them, and re-layouts  220 us (15%)
  matrix products  75.3 us (5%)
  other arithmetic  34.7 us (2%)
  between operations  15.5 us (1%)
    unnamed x24, waiting for transfers between devices  333 us
    reduce_scatter x1, waiting for transfers between devices, shards(): lax.psum_scatter(up_grad_weight, 'fsdp', scatter_dimension=0, tiled=True)  91.9 us
    reduce_scatter x1, waiting for transfers between devices, shards(): lax.psum_scatter(down_grad, 'fsdp', scatter_dimension=1, tiled=True)  91.9 us
    gather x2, local copies, waits for them, and re-layouts, pick_rows(): jnp.take_along_axis(values, safe_pos[:, :, None], axis=1)  83.5 us
    reduce_scatter x1, waiting for transfers between devices, shards(): lax.psum_scatter(query_grad_weight, 'fsdp', scatter_dimension=0, tiled=True)  66.8 us
    reduce_scatter x1, waiting for transfers between devices, shards(): lax.psum_scatter(value_grad_weight, 'fsdp', scatter_dimension=0, tiled=True)  66.3 us
    reduce_scatter x1, waiting for transfers between devices, shards(): lax.psum_scatter(key_grad_weight, 'fsdp', scatter_dimension=0, tiled=True)  66.2 us
    all_gather x1, waiting for transfers between devices, shards(): lax.all_gather(down_weight, 'fsdp', axis=1, tiled=True)  45 us
  transfers between devices with their start and end apart: 22, of which 16 were waited for; matrix products, arithmetic and copies ran while one was open for 7% of the time, Pallas kernels for 0%

profile of v1, /device:TPU:0, one launch (start us, length us, event | category | flops | bytes accessed | tf_op | source)
XLA Modules:
  0.0 1428.6 jit_solution(14199716306647410165)
XLA Ops:
  14.4 39.1 %gather_fusion = bf16[1024,1024]{1,0:T(8,128)(2,1)S(1)} fusion(bf16[8,256,1024]{2,1,0:T(8,128)(2,1)} %copy.187, s32[1024]{0:T(1024)S(1)} %or_bitcast_fusion), kind=kCustom, calls=%fused_computation.clone | custom fusion | bytes 4202496 | tf_op jit(solution)/shard_map/jit(take_along_axis)/gather | solution.py:17
  53.5 44.4 %gather_fusion.1 = bf16[1024,1024]{1,0:T(8,128)(2,1)} fusion(bf16[8,256,1024]{2,1,0:T(8,128)(2,1)} %copy.188, s32[1024]{0:T(1024)S(1)} %or_bitcast_fusion), kind=kCustom, calls=%fused_computation.1.clone | custom fusion | bytes 4202496 | tf_op jit(solution)/shard_map/jit(take_along_axis)/gather | solution.py:17
  110.0 21.5 %all-gather.1 = bf16[8,1,128]{2,1,0:T(2,128)(2,1)S(1)} all-gather(bf16[1,1,128]{2,1,0:T(2,128)(2,1)S(1)} %bitcast.219), channel_id=1, replica_groups=mesh['fsdp'=8,'tensor'=4] {'fsdp'}, dimensions={0}, use_global_device_ids=true | all-gather | bytes 2304 | tf_op jit(solution)/shard_map/all_gather | solution.py:110
  132.0 29.9 %all-reduce.17.cloned.1.call-done = bf16[8,32,4,1024]{3,1,2,0:T(8,128)(2,1)} async-done(((bf16[8,32,4,1024]{3,1,2,0:T(8,128)(2,1)}), bf16[8,32,4,1024]{3,1,2,0:T(8,128)(2,1)}) %all-reduce.17.cloned.1.call-update) | async-done | bytes 2097168
  167.3 31.6 %all_gather.59 = bf16[1024,256]{1,0:T(8,128)(2,1)S(1)} all-gather(bf16[128,256]{1,0:T(8,128)(2,1)S(1)} %copy-done.21), channel_id=1, replica_groups=mesh['fsdp'=8,'tensor'=4] {'fsdp'}, dimensions={0}, use_global_device_ids=true | all-gather | bytes 589824 | tf_op jit(solution)/shard_map/all_gather | solution.py:103
  198.8 31.9 %all_gather.60 = bf16[1024,256]{1,0:T(8,128)(2,1)S(1)} all-gather(bf16[128,256]{1,0:T(8,128)(2,1)S(1)} %copy-done.22), channel_id=1, replica_groups=mesh['fsdp'=8,'tensor'=4] {'fsdp'}, dimensions={0}, use_global_device_ids=true | all-gather | bytes 589824 | tf_op jit(solution)/shard_map/all_gather | solution.py:104
  236.2 33.6 %all_gather.61 = bf16[256,1024]{1,0:T(8,128)(2,1)} all-gather(bf16[256,128]{1,0:T(8,128)(2,1)S(1)} %copy-done.23), channel_id=1, replica_groups=mesh['fsdp'=8,'tensor'=4] {'fsdp'}, dimensions={1}, use_global_device_ids=true | all-gather | bytes 589824 | tf_op jit(solution)/shard_map/all_gather | solution.py:106
  297.0 16.1 %all-gather.2 = bf16[8,1,128]{2,1,0:T(2,128)(2,1)S(1)} all-gather(bf16[1,1,128]{2,1,0:T(2,128)(2,1)S(1)} %bitcast.220), channel_id=1, replica_groups=mesh['fsdp'=8,'tensor'=4] {'fsdp'}, dimensions={0}, use_global_device_ids=true | all-gather | bytes 2304 | tf_op jit(solution)/shard_map/all_gather | solution.py:111
  313.2 66.1 %all-reduce.19.cloned.1.call-done = f32[8,32,4,1024]{3,1,2,0:T(8,128)} async-done(((f32[8,32,4,1024]{3,1,2,0:T(8,128)}), f32[8,32,4,1024]{3,1,2,0:T(8,128)}) %all-reduce.19.cloned.1.call-update) | async-done | bytes 4194320
  388.0 17.4 %all-gather.15.cloned.1.call-done = bf16[8,32,4,1024]{3,1,2,0:T(8,128)(2,1)} async-done(((bf16[8,32,1,1024]{3,1,2,0:T(8,128)(2,1)}), bf16[8,32,4,1024]{3,1,2,0:T(8,128)(2,1)}) %all-gather.15.cloned.1.call-update) | async-done | bytes 2097168 | tf_op jit(solution)/shard_map/all_gather | solution.py:168
  414.0 42.7 %all-gather.17.cloned.1.call-done = bf16[1024,1024]{1,0:T(8,128)(2,1)} async-done(((bf16[128,1024]{1,0:T(8,128)(2,1)}), bf16[1024,1024]{1,0:T(8,128)(2,1)}) %all-gather.17.cloned.1.call-update) | async-done | bytes 2097168 | tf_op jit(solution)/shard_map/all_gather | solution.py:107
  463.1 45.0 %all-gather.19.cloned.1.call-done = bf16[1024,1024]{1,0:T(8,128)(2,1)} async-done(((bf16[1024,128]{1,0:T(8,128)(2,1)}), bf16[1024,1024]{1,0:T(8,128)(2,1)}) %all-gather.19.cloned.1.call-update) | async-done | bytes 2097168 | tf_op jit(solution)/shard_map/all_gather | solution.py:108
  523.6 17.6 %all-gather = bf16[8,1,128]{2,1,0:T(2,128)(2,1)S(1)} all-gather(bf16[1,1,128]{2,1,0:T(2,128)(2,1)S(1)} %bitcast.221), channel_id=1, replica_groups=mesh['fsdp'=8,'tensor'=4] {'fsdp'}, dimensions={0}, use_global_device_ids=true | all-gather | bytes 2304 | tf_op jit(solution)/shard_map/all_gather | solution.py:109
  542.4 64.5 %all-reduce.25.cloned.1.call-done = (bf16[8,32,4,1024]{3,1,2,0:T(8,128)(2,1)}, bf16[8,32,4,1024]{3,1,2,0:T(8,128)(2,1)}) async-done(((bf16[8,32,4,1024]{3,1,2,0:T(8,128)(2,1)}, bf16[8,32,4,1024]{3,1,2,0:T(8,128)(2,1)}), (bf16[8,32,4,1024]{3,1,2,0:T(8,128)(2,1)}, bf16[8,32,4,1024]{3,1,2,0:T(8,128)(2,1)})) %all-reduce.25.cloned.1.call-update) | async-done | bytes 4194320
  612.5 22.6 %all-gather.23.cloned.1.call-done = bf16[8,32,4,1024]{3,1,2,0:T(8,128)(2,1)} async-done(((bf16[8,32,1,1024]{3,1,2,0:T(8,128)(2,1)}), bf16[8,32,4,1024]{3,1,2,0:T(8,128)(2,1)}) %all-gather.23.cloned.1.call-update) | async-done | bytes 2097168 | tf_op jit(solution)/shard_map/all_gather | solution.py:217
  669.2 85.6 %all-reduce.21.cloned.1.call-done = f32[8,32,4,1024]{3,1,2,0:T(8,128)} async-done(((f32[8,32,4,1024]{3,1,2,0:T(8,128)}), f32[8,32,4,1024]{3,1,2,0:T(8,128)}) %all-reduce.21.cloned.1.call-update) | async-done | bytes 4194320
  760.3 33.8 %all_gather.69 = bf16[1024,256]{1,0:T(8,128)(2,1)} all-gather(bf16[128,256]{1,0:T(8,128)(2,1)S(1)} %copy-done.20), channel_id=1, replica_groups=mesh['fsdp'=8,'tensor'=4] {'fsdp'}, dimensions={0}, use_global_device_ids=true | all-gather | bytes 589824 | tf_op jit(solution)/shard_map/all_gather | solution.py:194
  833.7 85.7 %all-reduce.23.cloned.1.call-done = f32[8,32,4,1024]{3,1,2,0:T(8,128)} async-done(((f32[8,32,4,1024]{3,1,2,0:T(8,128)}), f32[8,32,4,1024]{3,1,2,0:T(8,128)}) %all-reduce.23.cloned.1.call-update) | async-done | bytes 4194320
  960.7 37.5 %all-reduce.9 = (f32[1024]{0:T(1024)S(1)}, f32[1024]{0:T(1024)S(1)}, f32[1024]{0:T(1024)S(1)}) all-reduce(f32[1024]{0:T(1024)S(1)} %bitcast.217, f32[1024]{0:T(1024)S(1)} %bitcast.216, f32[1024]{0:T(1024)S(1)} %bitcast.215), channel_id=14, replica_groups=mesh['fsdp'=8,'tensor'=4] {'fsdp'}, use_global_device_ids=true, to_apply=%region_26.28.clone | all-reduce | flops 3072 | bytes 24576
  1038.7 66.3 %reduce-scatter.29.cloned.1.call-done = f32[128,256]{1,0:T(8,128)} async-done(((f32[1024,256]{1,0:T(8,128)}), f32[128,256]{1,0:T(8,128)}) %reduce-scatter.29.cloned.1.call-update) | async-done | bytes 131088 | tf_op jit(solution)/shard_map/reduce_scatter | solution.py:314
  1105.0 66.8 %reduce-scatter.25.cloned.1.call-done = f32[128,256]{1,0:T(8,128)} async-done(((f32[1024,256]{1,0:T(8,128)}), f32[128,256]{1,0:T(8,128)}) %reduce-scatter.25.cloned.1.call-update) | async-done | bytes 131088 | tf_op jit(solution)/shard_map/reduce_scatter | solution.py:312
  1171.8 66.2 %reduce-scatter.27.cloned.1.call-done = f32[128,256]{1,0:T(8,128)} async-done(((f32[1024,256]{1,0:T(8,128)}), f32[128,256]{1,0:T(8,128)}) %reduce-scatter.27.cloned.1.call-update) | async-done | bytes 131088 | tf_op jit(solution)/shard_map/reduce_scatter | solution.py:313
  1238.0 91.9 %reduce-scatter.35.cloned.1.call-done = f32[1024,128]{1,0:T(8,128)} async-done(((f32[1024,1024]{1,0:T(8,128)}), f32[1024,128]{1,0:T(8,128)}) %reduce-scatter.35.cloned.1.call-update) | async-done | bytes 524304 | tf_op jit(solution)/shard_map/reduce_scatter | solution.py:317
  1329.9 91.9 %reduce-scatter.33.cloned.1.call-done = f32[128,1024]{1,0:T(8,128)} async-done(((f32[1024,1024]{1,0:T(8,128)}), f32[128,1024]{1,0:T(8,128)}) %reduce-scatter.33.cloned.1.call-update) | async-done | bytes 524304 | tf_op jit(solution)/shard_map/reduce_scatter | solution.py:316
  (228 shorter events, 263.4 us)
Async XLA Ops:
  7.2 154.8 %all-reduce.17.cloned.1.call-start = ((), (), s32[]{:S(2)}) async-start(), calls=%async_computation.20 | async-start | bytes 4194304
  109.3 89.5 %copy-start.22 = (bf16[128,256]{1,0:T(8,128)(2,1)S(1)}, bf16[128,256]{1,0:T(8,128)(2,1)}, u32[]{:S(2)}) copy-start(bf16[128,256]{1,0:T(8,128)(2,1)} %param.18) | copy-start | bytes 196612
  109.3 160.5 %all-gather.13.cloned.1.call-start = ((), (), s32[]{:S(2)}) async-start(), calls=%async_computation.6 | async-start | bytes 2621440 | tf_op jit(solution)/shard_map/all_gather | solution.py:128
  165.7 213.6 %all-reduce.19.cloned.1.call-start = ((), (), s32[]{:S(2)}) async-start(), calls=%async_computation.21 | async-start | bytes 8388608
  165.7 65.0 %collective-permute-start = (bf16[128,256]{1,0:T(8,128)(2,1)S(1)}, bf16[128,256]{1,0:T(8,128)(2,1)S(1)}, u32[]{:S(2)}, u32[]{:S(2)}) collective-permute-start(bf16[128,256]{1,0:T(8,128)(2,1)S(1)} %copy-done.19), channel_id=1, source_target_pairs={{0,4},{4,0},{8,12},{12,8},{16,20},{20,16},{24,28},{28,24},{1,5},{5... | collective-permute-start | bytes 196616 | tf_op jit(solution)/shard_map/ppermute | solution.py:95
  230.8 5.0 collective-permute-start.1
  235.9 39.2 %collective-permute-start.2 = (bf16[512,256]{1,0:T(8,128)(2,1)S(1)}, bf16[512,256]{1,0:T(8,128)(2,1)}, u32[]{:S(2)}, u32[]{:S(2)}) collective-permute-start(bf16[512,256]{1,0:T(8,128)(2,1)S(1)} %maximum_select_fusion.2), channel_id=1, source_target_pairs={{0,16},{4,20},{8,24},{12,28},{16,0},{20,4},{24,8},{28,12},{1,17},{... | collective-permute-start | bytes 786440 | tf_op jit(solution)/shard_map/ppermute | solution.py:95
  296.4 108.9 %all-gather.15.cloned.1.call-start = ((), (), s32[]{:S(2)}) async-start(), calls=%async_computation.7 | async-start | bytes 2621440 | tf_op jit(solution)/shard_map/all_gather | solution.py:168
  382.5 74.2 %all-gather.17.cloned.1.call-start = ((), (), s32[]{:S(2)}) async-start(), calls=%async_computation.8 | async-start | bytes 2359296 | tf_op jit(solution)/shard_map/all_gather | solution.py:107
  383.0 125.1 %all-gather.19.cloned.1.call-start = ((), (), s32[]{:S(2)}) async-start(), calls=%async_computation.9 | async-start | bytes 2359296 | tf_op jit(solution)/shard_map/all_gather | solution.py:108
  383.6 223.3 %all-reduce.25.cloned.1.call-start = ((), (), s32[]{:S(2)}) async-start(), calls=%async_computation.24 | async-start | bytes 8388608
  522.9 112.1 %all-gather.23.cloned.1.call-start = ((), (), s32[]{:S(2)}) async-start(), calls=%async_computation.11 | async-start | bytes 2621440 | tf_op jit(solution)/shard_map/all_gather | solution.py:217
  612.2 142.6 %all-reduce.21.cloned.1.call-start = ((), (), s32[]{:S(2)}) async-start(), calls=%async_computation.22 | async-start | bytes 8388608
  669.1 125.0 %all-gather.25.cloned.1.call-start = ((), (), s32[]{:S(2)}) async-start(), calls=%async_computation.12 | async-start | bytes 2621440 | tf_op jit(solution)/shard_map/all_gather | solution.py:236
  760.3 159.1 %all-reduce.23.cloned.1.call-start = ((), (), s32[]{:S(2)}) async-start(), calls=%async_computation.23 | async-start | bytes 8388608
  833.5 85.9 %copy-start.1 = (bf16[8,32,1,1024]{3,1,2,0:T(8,128)(2,1)S(1)}, bf16[8,32,1,1024]{3,1,2,0:T(8,128)(2,1)}, u32[]{:S(2)}) copy-start(bf16[8,32,1,1024]{3,1,2,0:T(8,128)(2,1)} %copy-done) | copy-start | bytes 1572868
  833.5 166.4 %all-gather.21.cloned.1.call-start = ((), (), s32[]{:S(2)}) async-start(), calls=%async_computation.10 | async-start | bytes 2621440 | tf_op jit(solution)/shard_map/all_gather | solution.py:186
  923.1 84.0 %all-gather.27.cloned.1.call-start = ((), (), s32[]{:S(2)}) async-start(), calls=%async_computation.13 | async-start | bytes 2621440 | tf_op jit(solution)/shard_map/all_gather | solution.py:304
  927.3 111.4 %reduce-scatter.31.cloned.1.call-start = ((), (), s32[]{:S(2)}) async-start(), calls=%async_computation.17 | async-start | bytes 1179648 | tf_op jit(solution)/shard_map/reduce_scatter | solution.py:315
  931.3 173.8 %reduce-scatter.29.cloned.1.call-start = ((), (), s32[]{:S(2)}) async-start(), calls=%async_computation.16 | async-start | bytes 1179648 | tf_op jit(solution)/shard_map/reduce_scatter | solution.py:314
  934.2 237.6 %reduce-scatter.25.cloned.1.call-start = ((), (), s32[]{:S(2)}) async-start(), calls=%async_computation.14 | async-start | bytes 1179648 | tf_op jit(solution)/shard_map/reduce_scatter | solution.py:312
  936.0 302.0 %reduce-scatter.27.cloned.1.call-start = ((), (), s32[]{:S(2)}) async-start(), calls=%async_computation.15 | async-start | bytes 1179648 | tf_op jit(solution)/shard_map/reduce_scatter | solution.py:313
  937.8 392.1 %reduce-scatter.35.cloned.1.call-start = ((), (), s32[]{:S(2)}) async-start(), calls=%async_computation.19 | async-start | bytes 4718592 | tf_op jit(solution)/shard_map/reduce_scatter | solution.py:317
  945.6 476.2 %reduce-scatter.33.cloned.1.call-start = ((), (), s32[]{:S(2)}) async-start(), calls=%async_computation.18 | async-start | bytes 4718592 | tf_op jit(solution)/shard_map/reduce_scatter | solution.py:316
  (32 other events, 410.5 us)
Sparse Core Ops, SparseCore 0:
  109.5 52.4 all-reduce.16
  165.8 22.6 all-gather.12
  296.5 82.6 all-reduce.18
  382.6 22.7 all-gather.14
  407.3 49.2 all-gather.16
  458.5 49.5 all-gather.18
  523.1 83.8 all-reduce.24
  612.3 22.7 all-gather.22
  669.3 85.4 all-reduce.20
  760.4 22.7 all-gather.24
  833.6 85.6 all-reduce.22
  923.3 22.7 all-gather.20
  947.7 22.9 all-gather.26
  974.9 63.8 reduce-scatter.30
  1042.5 62.4 reduce-scatter.28
  1109.3 62.5 reduce-scatter.24
  1175.6 62.3 reduce-scatter.26
  1242.5 87.3 reduce-scatter.34
  1334.1 87.6 reduce-scatter.32
